TPU v7x, 32 devices: a whole 2x2x4 slice. The times are simulated.
32 devices in a mesh: lat: 8 (over z, y), lev: 4 (over x, core).
Axes of the slice: x: 2, y: 2, z: 4, core: 2. Of those that a mesh axis runs over, the one named last changes fastest.
Arguments:
- tracer: float32 [2, 4, 384, 1152], P(None, 'lev', 'lat'), may hold values from 0.1 to 2
- east_courant: float32 [4, 384, 1152], P('lev', 'lat'), may hold values from -0.8 to 0.8
- north_courant: float32 [4, 384, 1152], P('lev', 'lat'), may hold values from -0.8 to 0.8
- fall_speed: float32 [2, 4, 384, 1152], P(None, 'lev', 'lat'), may hold values from 0.05 to 0.6
Outputs:
- tracer_out: float32 [2, 4, 384, 1152], P(None, 'lev', 'lat')
- deposit: float32 [2, 384, 1152], P(None, 'lat', 'lev')
All inputs are finite; a program needn't handle non-finite values.
Results may differ from a plain program's by a relative error of at most 0.0003.
Values sent between devices are 32-bit elements; how exact they have to be, the bound alone decides.
No kernel may reach another device: no remote copies, remote signals or barrier semaphores. Data moves between devices by JAX's collectives and lax.ppermute only.
A program may use at most 64 MiB of HBM per device.

v0:
```python
import jax
import jax.numpy as jnp
from jax import lax
from jax.sharding import PartitionSpec as P

HSUB = 4
SETTLE_SUBSTEPS = 6


def passed_along(block, axis, distance):
    devices = range(lax.axis_size(axis))
    route = [(i - distance, i) for i in devices if i - distance in devices]
    return lax.ppermute(block, axis, route)


def extended(block, sides, width):
    for axis, dim in sides:
        count = lax.axis_size(axis)
        forward = [(i, i + 1) for i in range(count - 1)]
        backward = [(target, source) for source, target in forward]
        low = lax.ppermute(
            lax.slice_in_dim(block, block.shape[dim] - width, None, axis=dim), axis, forward
        )
        high = lax.ppermute(lax.slice_in_dim(block, 0, width, axis=dim), axis, backward)
        block = jnp.concatenate([low, block, high], axis=dim)
    return block


def limiter_face_value(outer_west, inner_west, inner_east, outer_east):
    interp = 7.0 / 12.0 * (inner_west + inner_east) - 1.0 / 12.0 * (outer_west + outer_east)
    return jnp.clip(
        interp, jnp.minimum(inner_west, inner_east), jnp.maximum(inner_west, inner_east)
    )


def window_for_cell(source, start, length, axis_dim):
    return lax.slice_in_dim(source, start, start + length, axis=axis_dim)


def sweep(halo_padded_field, courant, axis_dim):
    cells = halo_padded_field.shape[axis_dim] - 6
    faces = limiter_face_value(
        window_for_cell(halo_padded_field, 0, cells + 3, axis_dim),
        window_for_cell(halo_padded_field, 1, cells + 3, axis_dim),
        window_for_cell(halo_padded_field, 2, cells + 3, axis_dim),
        window_for_cell(halo_padded_field, 3, cells + 3, axis_dim),
    )
    middle = window_for_cell(halo_padded_field, 2, cells + 2, axis_dim)
    west_face = window_for_cell(faces, 0, cells + 2, axis_dim)
    east_face = window_for_cell(faces, 1, cells + 2, axis_dim)
    spread = east_face - west_face
    curvature = 6.0 * middle - 3.0 * (west_face + east_face)
    courant_abs = jnp.abs(courant)
    shape_term = 1.0 - 2.0 / 3.0 * courant_abs
    from_west = window_for_cell(east_face, 0, cells + 1, axis_dim) - 0.5 * courant_abs * (
        window_for_cell(spread, 0, cells + 1, axis_dim)
        - shape_term * window_for_cell(curvature, 0, cells + 1, axis_dim)
    )
    from_east = window_for_cell(west_face, 1, cells + 1, axis_dim) + 0.5 * courant_abs * (
        window_for_cell(spread, 1, cells + 1, axis_dim)
        + shape_term * window_for_cell(curvature, 1, cells + 1, axis_dim)
    )
    face_flux_values = courant * jnp.where(courant >= 0, from_west, from_east)
    return window_for_cell(halo_padded_field, 3, cells, axis_dim) - (
        window_for_cell(face_flux_values, 1, cells, axis_dim)
        - window_for_cell(face_flux_values, 0, cells, axis_dim)
    )


def zonal(field, east_courant):
    last_dim = field.ndim - 1
    width = field.shape[last_dim]
    halo_padded_field = jnp.concatenate(
        [
            window_for_cell(field, width - 3, 3, last_dim),
            field,
            window_for_cell(field, 0, 3, last_dim),
        ],
        last_dim,
    )
    cour_dim = east_courant.ndim - 1
    courant = jnp.concatenate(
        [window_for_cell(east_courant, width - 1, 1, cour_dim), east_courant], cour_dim
    )
    return sweep(halo_padded_field, courant, last_dim)


def settle_flat(column_mass, fall_speed):
    deposit = jnp.zeros_like(column_mass[:, 0])
    for settle_substep in range(SETTLE_SUBSTEPS):
        speeds = fall_speed * (1.0 + 0.5 * jnp.tanh(column_mass))
        face_flux_values = speeds * column_mass
        inflow = jnp.concatenate(
            [jnp.zeros_like(face_flux_values[:, :1]), face_flux_values[:, :-1]], 1
        )
        column_mass = column_mass + inflow - face_flux_values
        deposit = deposit + face_flux_values[:, -1]
    return (column_mass, deposit)


def columns_settle(split_portions):
    column_mass, speed_piece = split_portions
    shape_full = column_mass.shape
    flat_shape = (shape_full[0], shape_full[1], shape_full[2] * shape_full[3])
    settled, deposit = settle_flat(column_mass.reshape(flat_shape), speed_piece.reshape(flat_shape))
    returned = lax.all_to_all(
        settled.reshape(shape_full), "lev", split_axis=1, concat_axis=3, tiled=True
    )
    return (returned, deposit.reshape((shape_full[0], shape_full[2], shape_full[3])))


def on_device(tracer, east_courant, north_courant, fall_speed):
    band_rows = tracer.shape[2]
    all_rows = band_rows * lax.axis_size("lat")
    first_row = lax.axis_index("lat") * band_rows
    row_ids = first_row + jnp.arange(band_rows, dtype=jnp.int32)
    north_faces = jnp.where(
        (row_ids == all_rows - 1)[None, :, None], jnp.zeros_like(north_courant), north_courant
    )
    southern_row = passed_along(north_faces[:, band_rows - 1 :, :], "lat", 1)
    face_cour = jnp.concatenate([southern_row, north_faces], 1)
    field = tracer
    for settle_substep in range(HSUB):
        field = zonal(field, east_courant)
        halo_padded_field = extended(field, (("lat", 2),), 3)
        field = sweep(halo_padded_field, face_cour, 2)
    field, deposit = columns_settle(
        (
            lax.all_to_all(field, "lev", split_axis=3, concat_axis=1, tiled=True),
            lax.all_to_all(fall_speed, "lev", split_axis=3, concat_axis=1, tiled=True),
        )
    )
    field = zonal(field, east_courant)
    halo_padded_field = extended(field, (("lat", 2),), 3)
    field = sweep(halo_padded_field, face_cour, 2)
    return (field, deposit)


def solution(mesh):
    in_specs = (
        P(None, "lev", "lat", None),
        P("lev", "lat", None),
        P("lev", "lat", None),
        P(None, "lev", "lat", None),
    )
    out_specs = (P(None, "lev", "lat", None), P(None, "lat", "lev"))
    return jax.shard_map(
        on_device, mesh=mesh, in_specs=in_specs, out_specs=out_specs, check_vma=False
    )
```

profile of v0, /device:TPU:0, one launch (start us, length us, event | category | flops | bytes accessed | tf_op | source)
XLA Modules:
  0.0 129.7 jit_solution(10379016936662951680)
XLA Ops:
  1.8 4.9 %collective-permute-start = (f32[1,1,1152]{2,1,0:T(1,128)S(1)}, f32[1,1,1152]{2,1,0:T(1,128)S(1)}, u32[]{:S(2)}, u32[]{:S(2)}) collective-permute-start(f32[1,1,1152]{2,1,0:T(1,128)S(1)} %slice.702), channel_id=1, source_target_pairs={{0,4},{4,8},{8,12},{12,16},{16,20},{20,24},{24,28},{1,5},{5,9},{9,... | collective-permute-start | bytes 13832 | tf_op jit(solution)/shard_map/ppermute | solution.py:13
  11.7 3.4 %collective-permute-start.1 = (f32[2,1,3,1152]{3,2,1,0:T(4,128)S(1)}, f32[2,1,3,1152]{3,2,1,0:T(4,128)S(1)}, u32[]{:S(2)}, u32[]{:S(2)}) collective-permute-start(f32[2,1,3,1152]{3,2,1,0:T(4,128)S(1)} %get-tuple-element.46), channel_id=1, source_target_pairs={{0,4},{4,8},{8,12},{12,16},{16,20},{20,24},{24,28},{1,5},{5,9},{9,... | collective-permute-start | bytes 82952 | tf_op jit(solution)/shard_map/ppermute | solution.py:21
  16.7 4.2 %collective-permute-done.2 = f32[2,1,3,1152]{3,2,1,0:T(4,128)S(1)} collective-permute-done((f32[2,1,3,1152]{3,2,1,0:T(4,128)S(1)}, f32[2,1,3,1152]{3,2,1,0:T(4,128)S(1)}, u32[]{:S(2)}, u32[]{:S(2)}) %collective-permute-start.2) | collective-permute-done | bytes 27680 | tf_op jit(solution)/shard_map/ppermute | solution.py:24
  23.7 4.3 %collective-permute-start.3 = (f32[2,1,3,1152]{3,2,1,0:T(4,128)S(1)}, f32[2,1,3,1152]{3,2,1,0:T(4,128)S(1)}, u32[]{:S(2)}, u32[]{:S(2)}) collective-permute-start(f32[2,1,3,1152]{3,2,1,0:T(4,128)S(1)} %get-tuple-element.42), channel_id=1, source_target_pairs={{0,4},{4,8},{8,12},{12,16},{16,20},{20,24},{24,28},{1,5},{5,9},{9,... | collective-permute-start | bytes 82952 | tf_op jit(solution)/shard_map/ppermute | solution.py:21
  29.6 4.2 %collective-permute-done.4 = f32[2,1,3,1152]{3,2,1,0:T(4,128)S(1)} collective-permute-done((f32[2,1,3,1152]{3,2,1,0:T(4,128)S(1)}, f32[2,1,3,1152]{3,2,1,0:T(4,128)S(1)}, u32[]{:S(2)}, u32[]{:S(2)}) %collective-permute-start.4) | collective-permute-done | bytes 27680 | tf_op jit(solution)/shard_map/ppermute | solution.py:24
  36.6 3.4 %collective-permute-start.5 = (f32[2,1,3,1152]{3,2,1,0:T(4,128)S(1)}, f32[2,1,3,1152]{3,2,1,0:T(4,128)S(1)}, u32[]{:S(2)}, u32[]{:S(2)}) collective-permute-start(f32[2,1,3,1152]{3,2,1,0:T(4,128)S(1)} %get-tuple-element.38), channel_id=1, source_target_pairs={{0,4},{4,8},{8,12},{12,16},{16,20},{20,24},{24,28},{1,5},{5,9},{9,... | collective-permute-start | bytes 82952 | tf_op jit(solution)/shard_map/ppermute | solution.py:21
  41.8 4.1 %collective-permute-done.6 = f32[2,1,3,1152]{3,2,1,0:T(4,128)S(1)} collective-permute-done((f32[2,1,3,1152]{3,2,1,0:T(4,128)S(1)}, f32[2,1,3,1152]{3,2,1,0:T(4,128)S(1)}, u32[]{:S(2)}, u32[]{:S(2)}) %collective-permute-start.6) | collective-permute-done | bytes 27680 | tf_op jit(solution)/shard_map/ppermute | solution.py:24
  48.6 4.3 %collective-permute-start.7 = (f32[2,1,3,1152]{3,2,1,0:T(4,128)S(1)}, f32[2,1,3,1152]{3,2,1,0:T(4,128)S(1)}, u32[]{:S(2)}, u32[]{:S(2)}) collective-permute-start(f32[2,1,3,1152]{3,2,1,0:T(4,128)S(1)} %get-tuple-element.34), channel_id=1, source_target_pairs={{0,4},{4,8},{8,12},{12,16},{16,20},{20,24},{24,28},{1,5},{5,9},{9,... | collective-permute-start | bytes 82952 | tf_op jit(solution)/shard_map/ppermute | solution.py:21
  54.4 2.0 %copy.56 = f32[2,1,48,1152]{2,0,1,3:T(2,128)S(1)} copy(f32[2,1,48,1152]{3,2,1,0:T(8,128)} %param.7) | data formatting | bytes 884736 | tf_op args[3]
  56.4 2.9 %reshape.594 = f32[4,1,27648]{2,1,0:T(1,128)} reshape(f32[1152,1,2,48]{3,2,1,0:T(2,128)S(1)} %bitcast.40) | data formatting | bytes 884736
  59.3 4.1 %all-to-all-start.1 = ((f32[4,1,27648]{2,1,0:T(1,128)}), f32[4,1,27648]{2,1,0:T(1,128)}, u32[]{:S(2)}, u32[]{:S(2)}) async-start(f32[4,1,27648]{2,1,0:T(1,128)} %reshape.594), calls=%async_computation.1 | async-start | bytes 884736 | tf_op jit(solution)/shard_map/all_to_all | solution.py:130
  65.4 2.8 %reshape.596 = f32[4,1,27648]{2,1,0:T(1,128)} reshape(f32[1152,1,2,48]{3,2,1,0:T(2,128)S(1)} %bitcast.37) | data formatting | bytes 884736
  68.3 3.1 %all-to-all-done.1 = f32[4,1,27648]{2,1,0:T(1,128)} async-done(((f32[4,1,27648]{2,1,0:T(1,128)}), f32[4,1,27648]{2,1,0:T(1,128)}, u32[]{:S(2)}, u32[]{:S(2)}) %all-to-all-start.1) | async-done | bytes 442400 | tf_op jit(solution)/shard_map/all_to_all | solution.py:130
  71.4 4.1 %all-to-all-start = ((f32[4,1,27648]{2,1,0:T(1,128)}), f32[4,1,27648]{2,1,0:T(1,128)}, u32[]{:S(2)}, u32[]{:S(2)}) async-start(f32[4,1,27648]{2,1,0:T(1,128)} %reshape.596), calls=%async_computation | async-start | bytes 884736 | tf_op jit(solution)/shard_map/all_to_all | solution.py:129
  76.0 2.8 %reduce.2 = f32[4,27648]{1,0:T(4,128)S(1)} reduce(f32[4,1,27648]{2,1,0:T(1,128)} %all-to-all-done.1, f32[]{:T(128)} %broadcast.305), dimensions={1}, to_apply=%all_to_all.38.reduce_sub_computation | reduce | bytes 884740 | tf_op jit(solution)/shard_map/all_to_all | solution.py:130
  78.8 1.9 %reshape.595 = f32[1152,1,2,48]{3,2,1,0:T(2,128)S(1)} reshape(f32[4,27648]{1,0:T(4,128)S(1)} %reduce.2) | data formatting | bytes 884736
  81.8 1.7 %all-to-all-done = f32[4,1,27648]{2,1,0:T(1,128)} async-done(((f32[4,1,27648]{2,1,0:T(1,128)}), f32[4,1,27648]{2,1,0:T(1,128)}, u32[]{:S(2)}, u32[]{:S(2)}) %all-to-all-start) | async-done | bytes 442400 | tf_op jit(solution)/shard_map/all_to_all | solution.py:129
  83.5 3.6 %reduce.3 = f32[4,27648]{1,0:T(4,128)} reduce(f32[4,1,27648]{2,1,0:T(1,128)} %all-to-all-done, f32[]{:T(128)} %broadcast.305), dimensions={1}, to_apply=%all_to_all.35.reduce_sub_computation | reduce | bytes 884740 | tf_op jit(solution)/shard_map/all_to_all | solution.py:129
  87.1 2.9 %reshape.597 = f32[1152,1,2,48]{3,2,1,0:T(2,128)S(1)} reshape(f32[4,27648]{1,0:T(4,128)} %reduce.3) | data formatting | bytes 884736
  91.4 1.5 %reshape.589 = f32[2,4,13824]{2,1,0:T(4,128)S(1)} reshape(f32[2,4,1,48,288]{4,3,1,0,2:T(8,128)} %bitcast.48) | data formatting | bytes 884736 | tf_op jit(solution)/shard_map/reshape | solution.py:105
  98.0 2.3 %reshape.591 = f32[2,4,48,288]{3,2,1,0:T(8,128)} reshape(f32[2,4,13824]{2,1,0:T(4,128)} %add_subtract_fusion) | data formatting | bytes 884736 | tf_op jit(solution)/shard_map/reshape | solution.py:107
  101.4 11.9 %all_to_all.48 = f32[2,4,48,288]{3,2,0,1:T(8,128)S(1)} all-to-all(f32[2,4,48,288]{3,2,0,1:T(8,128)S(1)} %copy.58), channel_id=1, replica_groups=mesh['lat'=8,'lev'=4] {'lev'}, dimensions={1} | all-to-all | bytes 884736 | tf_op jit(solution)/shard_map/all_to_all | solution.py:106
  117.7 4.5 %collective-permute-start.9 = (f32[2,1,3,1152]{3,2,1,0:T(4,128)S(1)}, f32[2,1,3,1152]{3,2,1,0:T(4,128)S(1)}, u32[]{:S(2)}, u32[]{:S(2)}) collective-permute-start(f32[2,1,3,1152]{3,2,1,0:T(4,128)S(1)} %get-tuple-element.30), channel_id=1, source_target_pairs={{0,4},{4,8},{8,12},{12,16},{16,20},{20,24},{24,28},{1,5},{5,9},{9,... | collective-permute-start | bytes 82952 | tf_op jit(solution)/shard_map/ppermute | solution.py:21
  123.5 2.3 %fusion.142 = f32[2,13824]{1,0:T(2,128)S(1)} fusion(f32[2,4,13824]{2,1,0:T(4,128)} %copy-done.4, f32[2,4,13824]{2,1,0:T(4,128)} %copy-done, f32[2,4,13824]{2,1,0:T(4,128)} %copy-done.3, f32[2,4,13824]{2,1,0:T(4,128)S(1)} %get-tuple-element.8, f32[2,4,13824]{2,1,0:T(4,128)} %copy-done.2, f32[2,4,13824]{2,1,0:T(4,128)S(1)} %multiply_multiply_fusion.5), kind=kLoop, calls=%fused_computation.228 | loop fusion | flops 138240 | bytes 774144 | tf_op jit(solution)/shard_map/add | solution.py:97
  (114 shorter events, 41.1 us)
Async XLA Ops:
  0.6 9.1 %copy-start.5 = (f32[1,48,1152]{2,1,0:T(8,128)S(1)}, f32[1,48,1152]{2,1,0:T(8,128)}, u32[]{:S(2)}) copy-start(f32[1,48,1152]{2,1,0:T(8,128)} %param.5) | copy-start | bytes 663556
  0.6 9.0 %copy-start.1 = (f32[2,1,48,1152]{3,2,1,0:T(8,128)S(1)}, f32[2,1,48,1152]{3,2,1,0:T(8,128)}, u32[]{:S(2)}) copy-start(f32[2,1,48,1152]{3,2,1,0:T(8,128)} %param.4) | copy-start | bytes 1327108
  1.8 14.7 %collective-permute-start = (f32[1,1,1152]{2,1,0:T(1,128)S(1)}, f32[1,1,1152]{2,1,0:T(1,128)S(1)}, u32[]{:S(2)}, u32[]{:S(2)}) collective-permute-start(f32[1,1,1152]{2,1,0:T(1,128)S(1)} %slice.702), channel_id=1, source_target_pairs={{0,4},{4,8},{8,12},{12,16},{16,20},{20,24},{24,28},{1,5},{5,9},{9,... | collective-permute-start | bytes 13832 | tf_op jit(solution)/shard_map/ppermute | solution.py:13
  11.4 5.0 %copy-start.6 = (f32[1,48,1152]{2,1,0:T(8,128)S(1)}, f32[1,48,1152]{2,1,0:T(8,128)}, u32[]{:S(2)}) copy-start(f32[1,48,1152]{2,1,0:T(8,128)} %param.6) | copy-start | bytes 663556
  11.7 5.1 %collective-permute-start.1 = (f32[2,1,3,1152]{3,2,1,0:T(4,128)S(1)}, f32[2,1,3,1152]{3,2,1,0:T(4,128)S(1)}, u32[]{:S(2)}, u32[]{:S(2)}) collective-permute-start(f32[2,1,3,1152]{3,2,1,0:T(4,128)S(1)} %get-tuple-element.46), channel_id=1, source_target_pairs={{0,4},{4,8},{8,12},{12,16},{16,20},{20,24},{24,28},{1,5},{5,9},{9,... | collective-permute-start | bytes 82952 | tf_op jit(solution)/shard_map/ppermute | solution.py:21
  15.1 5.9 %collective-permute-start.2 = (f32[2,1,3,1152]{3,2,1,0:T(4,128)S(1)}, f32[2,1,3,1152]{3,2,1,0:T(4,128)S(1)}, u32[]{:S(2)}, u32[]{:S(2)}) collective-permute-start(f32[2,1,3,1152]{3,2,1,0:T(4,128)S(1)} %get-tuple-element.47), channel_id=1, source_target_pairs={{4,0},{8,4},{12,8},{16,12},{20,16},{24,20},{28,24},{5,1},{9,5},{13... | collective-permute-start | bytes 82952 | tf_op jit(solution)/shard_map/ppermute | solution.py:24
  23.7 6.0 %collective-permute-start.3 = (f32[2,1,3,1152]{3,2,1,0:T(4,128)S(1)}, f32[2,1,3,1152]{3,2,1,0:T(4,128)S(1)}, u32[]{:S(2)}, u32[]{:S(2)}) collective-permute-start(f32[2,1,3,1152]{3,2,1,0:T(4,128)S(1)} %get-tuple-element.42), channel_id=1, source_target_pairs={{0,4},{4,8},{8,12},{12,16},{16,20},{20,24},{24,28},{1,5},{5,9},{9,... | collective-permute-start | bytes 82952 | tf_op jit(solution)/shard_map/ppermute | solution.py:21
  28.0 5.9 %collective-permute-start.4 = (f32[2,1,3,1152]{3,2,1,0:T(4,128)S(1)}, f32[2,1,3,1152]{3,2,1,0:T(4,128)S(1)}, u32[]{:S(2)}, u32[]{:S(2)}) collective-permute-start(f32[2,1,3,1152]{3,2,1,0:T(4,128)S(1)} %get-tuple-element.43), channel_id=1, source_target_pairs={{4,0},{8,4},{12,8},{16,12},{20,16},{24,20},{28,24},{5,1},{9,5},{13... | collective-permute-start | bytes 82952 | tf_op jit(solution)/shard_map/ppermute | solution.py:24
  36.6 5.2 %collective-permute-start.5 = (f32[2,1,3,1152]{3,2,1,0:T(4,128)S(1)}, f32[2,1,3,1152]{3,2,1,0:T(4,128)S(1)}, u32[]{:S(2)}, u32[]{:S(2)}) collective-permute-start(f32[2,1,3,1152]{3,2,1,0:T(4,128)S(1)} %get-tuple-element.38), channel_id=1, source_target_pairs={{0,4},{4,8},{8,12},{12,16},{16,20},{20,24},{24,28},{1,5},{5,9},{9,... | collective-permute-start | bytes 82952 | tf_op jit(solution)/shard_map/ppermute | solution.py:21
  40.0 5.9 %collective-permute-start.6 = (f32[2,1,3,1152]{3,2,1,0:T(4,128)S(1)}, f32[2,1,3,1152]{3,2,1,0:T(4,128)S(1)}, u32[]{:S(2)}, u32[]{:S(2)}) collective-permute-start(f32[2,1,3,1152]{3,2,1,0:T(4,128)S(1)} %get-tuple-element.39), channel_id=1, source_target_pairs={{4,0},{8,4},{12,8},{16,12},{20,16},{24,20},{28,24},{5,1},{9,5},{13... | collective-permute-start | bytes 82952 | tf_op jit(solution)/shard_map/ppermute | solution.py:24
  48.6 14.8 %collective-permute-start.7 = (f32[2,1,3,1152]{3,2,1,0:T(4,128)S(1)}, f32[2,1,3,1152]{3,2,1,0:T(4,128)S(1)}, u32[]{:S(2)}, u32[]{:S(2)}) collective-permute-start(f32[2,1,3,1152]{3,2,1,0:T(4,128)S(1)} %get-tuple-element.34), channel_id=1, source_target_pairs={{0,4},{4,8},{8,12},{12,16},{16,20},{20,24},{24,28},{1,5},{5,9},{9,... | collective-permute-start | bytes 82952 | tf_op jit(solution)/shard_map/ppermute | solution.py:21
  52.9 10.5 %collective-permute-start.8 = (f32[2,1,3,1152]{3,2,1,0:T(4,128)S(1)}, f32[2,1,3,1152]{3,2,1,0:T(4,128)S(1)}, u32[]{:S(2)}, u32[]{:S(2)}) collective-permute-start(f32[2,1,3,1152]{3,2,1,0:T(4,128)S(1)} %get-tuple-element.35), channel_id=1, source_target_pairs={{4,0},{8,4},{12,8},{16,12},{20,16},{24,20},{28,24},{5,1},{9,5},{13... | collective-permute-start | bytes 82952 | tf_op jit(solution)/shard_map/ppermute | solution.py:24
  59.3 12.1 %all-to-all-start.1 = ((f32[4,1,27648]{2,1,0:T(1,128)}), f32[4,1,27648]{2,1,0:T(1,128)}, u32[]{:S(2)}, u32[]{:S(2)}) async-start(f32[4,1,27648]{2,1,0:T(1,128)} %reshape.594), calls=%async_computation.1 | async-start | bytes 884736 | tf_op jit(solution)/shard_map/all_to_all | solution.py:130
  71.4 12.1 %all-to-all-start = ((f32[4,1,27648]{2,1,0:T(1,128)}), f32[4,1,27648]{2,1,0:T(1,128)}, u32[]{:S(2)}, u32[]{:S(2)}) async-start(f32[4,1,27648]{2,1,0:T(1,128)} %reshape.596), calls=%async_computation | async-start | bytes 884736 | tf_op jit(solution)/shard_map/all_to_all | solution.py:129
  93.5 0.8 copy-start.2
  94.7 0.8 copy-start.3
  95.5 2.6 %copy-start = (f32[2,4,13824]{2,1,0:T(4,128)}, f32[2,4,13824]{2,1,0:T(4,128)S(1)}, u32[]{:S(2)}) copy-start(f32[2,4,13824]{2,1,0:T(4,128)S(1)} %get-tuple-element.6) | copy-start | bytes 1327108
  95.9 0.8 copy-start.4
  117.7 9.0 %collective-permute-start.9 = (f32[2,1,3,1152]{3,2,1,0:T(4,128)S(1)}, f32[2,1,3,1152]{3,2,1,0:T(4,128)S(1)}, u32[]{:S(2)}, u32[]{:S(2)}) collective-permute-start(f32[2,1,3,1152]{3,2,1,0:T(4,128)S(1)} %get-tuple-element.30), channel_id=1, source_target_pairs={{0,4},{4,8},{8,12},{12,16},{16,20},{20,24},{24,28},{1,5},{5,9},{9,... | collective-permute-start | bytes 82952 | tf_op jit(solution)/shard_map/ppermute | solution.py:21
  122.2 5.9 %collective-permute-start.10 = (f32[2,1,3,1152]{3,2,1,0:T(4,128)S(1)}, f32[2,1,3,1152]{3,2,1,0:T(4,128)S(1)}, u32[]{:S(2)}, u32[]{:S(2)}) collective-permute-start(f32[2,1,3,1152]{3,2,1,0:T(4,128)S(1)} %get-tuple-element.31), channel_id=1, source_target_pairs={{4,0},{8,4},{12,8},{16,12},{20,16},{24,20},{28,24},{5,1},{9,5},{13... | collective-permute-start | bytes 82952 | tf_op jit(solution)/shard_map/ppermute | solution.py:24
where the time goes:
time: 131 us; the launch traced here: 130 us
  starting transfers between devices  39.9 us (30%)
  other arithmetic  28.9 us (22%)
  local copies, waits for them, and re-layouts  28.2 us (22%)
  waiting for transfers between devices  19.6 us (15%)
  blocking collectives  11.9 us (9%)
    ppermute x5, starting transfers between devices, extended(): lax.ppermute(lax.slice_in_dim(block, block.shape[dim] - width, None, axis...  20.1 us
    ppermute x5, waiting for transfers between devices, extended(): lax.ppermute(lax.slice_in_dim(block, 0, width, axis=dim), axis, backward)  14 us
    unnamed x19, local copies, waits for them, and re-layouts  13.3 us
    all_to_all x1, blocking collectives, columns_settle(): lax.all_to_all(settled.reshape(shape_full), 'lev', split_axis=1, concat_a...  11.9 us
    ppermute x5, starting transfers between devices, extended(): lax.ppermute(lax.slice_in_dim(block, 0, width, axis=dim), axis, backward)  6.64 us
    ppermute x1, starting transfers between devices, passed_along(): return lax.ppermute(block, axis, route)  4.9 us
    all_to_all x1, starting transfers between devices, on_device(): lax.all_to_all(fall_speed, 'lev', split_axis=3, concat_axis=1, tiled=True)  4.13 us
    all_to_all x1, starting transfers between devices, on_device(): lax.all_to_all(field, 'lev', split_axis=3, concat_axis=1, tiled=True)  4.12 us
  transfers between devices with their start and end apart: 13, of which 8 were waited for; matrix products, arithmetic and copies ran while one was open for 19% of the time, Pallas kernels for 0%

commit v1 on v0

--- a/solution.py
+++ b/solution.py
@@ -127,7 +127,15 @@
     field, deposit = columns_settle(
         (
             lax.all_to_all(field, "lev", split_axis=3, concat_axis=1, tiled=True),
-            lax.all_to_all(fall_speed, "lev", split_axis=3, concat_axis=1, tiled=True),
+            jnp.concatenate(
+                lax.all_to_all(
+                    jnp.stack(jnp.split(fall_speed, lax.axis_size("lev"), axis=3), axis=0),
+                    "lev",
+                    0,
+                    0,
+                ),
+                axis=1,
+            ),
         )
     )
     field = zonal(field, east_courant)

time: 131 us -> 127 us (0.969)
  local copies, waits for them, and re-layouts: 28.2 us -> 22.9 us
  waiting for transfers between devices: 19.6 us -> 24.7 us
  other arithmetic: 28.9 us -> 26.2 us
    unnamed x19 -> x20, local copies, waits for them, and re-layouts: 13.3 us -> 6.64 us
    all_to_all x1, waiting for transfers between devices: 1.67 us -> 6.28 us  [on_device(): lax.all_to_all(field, 'lev', split_axis=3, concat_axis=1, tiled=True)]
    all_to_all x1 -> x0, other arithmetic: 2.81 us -> none  [on_device(): lax.all_to_all(fall_speed, 'lev', split_axis=3, concat_axis=1, tiled=True)]
    another operation x0 -> x3, local copies, waits for them, and re-layouts: none -> 2.52 us  [the longest x1 1.62 us: columns_settle(): speed_piece.reshape(flat_shape)]
    all_to_all x1, waiting for transfers between devices: 3.09 us -> 4.5 us  [on_device(): lax.all_to_all(jnp.stack(jnp.split(fall_speed, lax.axis_size('lev'), axis...]
  transfers between devices with their start and end apart: 13 -> 13, of which waited for: 8 -> 7; matrix products, arithmetic and copies ran while one was open for 19% -> 13% of each run, Pallas kernels for 0% -> 0%
where the time goes in v1:
time: 127 us; the launch traced here: 126 us
  starting transfers between devices  39.2 us (31%)
  other arithmetic  26.2 us (21%)
  waiting for transfers between devices  24.7 us (19%)
  local copies, waits for them, and re-layouts  22.9 us (18%)
  blocking collectives  11.9 us (9%)
  between operations  1.29 us (1%)
    ppermute x5, starting transfers between devices, extended(): lax.ppermute(lax.slice_in_dim(block, block.shape[dim] - width, None, axis...  20.1 us
    ppermute x5, waiting for transfers between devices, extended(): lax.ppermute(lax.slice_in_dim(block, 0, width, axis=dim), axis, backward)  13.8 us
    all_to_all x1, blocking collectives, columns_settle(): lax.all_to_all(settled.reshape(shape_full), 'lev', split_axis=1, concat_a...  11.9 us
    unnamed x20, local copies, waits for them, and re-layouts  6.64 us
    ppermute x5, starting transfers between devices, extended(): lax.ppermute(lax.slice_in_dim(block, 0, width, axis=dim), axis, backward)  6.46 us
    all_to_all x1, waiting for transfers between devices, on_device(): lax.all_to_all(field, 'lev', split_axis=3, concat_axis=1, tiled=True)  6.28 us
    ppermute x1, starting transfers between devices, passed_along(): return lax.ppermute(block, axis, route)  4.9 us
    all_to_all x1, waiting for transfers between devices, on_device(): lax.all_to_all(jnp.stack(jnp.split(fall_speed, lax.axis_size('lev'), axis...  4.5 us
  transfers between devices with their start and end apart: 13, of which 7 were waited for; matrix products, arithmetic and copies ran while one was open for 13% of the time, Pallas kernels for 0%

profile of v1, /device:TPU:0, one launch (start us, length us, event | category | flops | bytes accessed | tf_op | source)
XLA Modules:
  0.0 126.3 jit_solution(12682020555665694493)
XLA Ops:
  1.8 4.9 %collective-permute-start = (f32[1,1,1152]{2,1,0:T(1,128)S(1)}, f32[1,1,1152]{2,1,0:T(1,128)S(1)}, u32[]{:S(2)}, u32[]{:S(2)}) collective-permute-start(f32[1,1,1152]{2,1,0:T(1,128)S(1)} %slice.702), channel_id=1, source_target_pairs={{0,4},{4,8},{8,12},{12,16},{16,20},{20,24},{24,28},{1,5},{5,9},{9,... | collective-permute-start | bytes 13832 | tf_op jit(solution)/shard_map/ppermute | solution.py:13
  11.7 3.4 %collective-permute-start.1 = (f32[2,1,3,1152]{3,2,1,0:T(4,128)S(1)}, f32[2,1,3,1152]{3,2,1,0:T(4,128)S(1)}, u32[]{:S(2)}, u32[]{:S(2)}) collective-permute-start(f32[2,1,3,1152]{3,2,1,0:T(4,128)S(1)} %get-tuple-element.46), channel_id=1, source_target_pairs={{0,4},{4,8},{8,12},{12,16},{16,20},{20,24},{24,28},{1,5},{5,9},{9,... | collective-permute-start | bytes 82952 | tf_op jit(solution)/shard_map/ppermute | solution.py:21
  16.8 4.2 %collective-permute-done.2 = f32[2,1,3,1152]{3,2,1,0:T(4,128)S(1)} collective-permute-done((f32[2,1,3,1152]{3,2,1,0:T(4,128)S(1)}, f32[2,1,3,1152]{3,2,1,0:T(4,128)S(1)}, u32[]{:S(2)}, u32[]{:S(2)}) %collective-permute-start.2) | collective-permute-done | bytes 27680 | tf_op jit(solution)/shard_map/ppermute | solution.py:24
  23.8 4.3 %collective-permute-start.3 = (f32[2,1,3,1152]{3,2,1,0:T(4,128)S(1)}, f32[2,1,3,1152]{3,2,1,0:T(4,128)S(1)}, u32[]{:S(2)}, u32[]{:S(2)}) collective-permute-start(f32[2,1,3,1152]{3,2,1,0:T(4,128)S(1)} %get-tuple-element.42), channel_id=1, source_target_pairs={{0,4},{4,8},{8,12},{12,16},{16,20},{20,24},{24,28},{1,5},{5,9},{9,... | collective-permute-start | bytes 82952 | tf_op jit(solution)/shard_map/ppermute | solution.py:21
  29.7 4.2 %collective-permute-done.4 = f32[2,1,3,1152]{3,2,1,0:T(4,128)S(1)} collective-permute-done((f32[2,1,3,1152]{3,2,1,0:T(4,128)S(1)}, f32[2,1,3,1152]{3,2,1,0:T(4,128)S(1)}, u32[]{:S(2)}, u32[]{:S(2)}) %collective-permute-start.4) | collective-permute-done | bytes 27680 | tf_op jit(solution)/shard_map/ppermute | solution.py:24
  36.7 3.4 %collective-permute-start.5 = (f32[2,1,3,1152]{3,2,1,0:T(4,128)S(1)}, f32[2,1,3,1152]{3,2,1,0:T(4,128)S(1)}, u32[]{:S(2)}, u32[]{:S(2)}) collective-permute-start(f32[2,1,3,1152]{3,2,1,0:T(4,128)S(1)} %get-tuple-element.38), channel_id=1, source_target_pairs={{0,4},{4,8},{8,12},{12,16},{16,20},{20,24},{24,28},{1,5},{5,9},{9,... | collective-permute-start | bytes 82952 | tf_op jit(solution)/shard_map/ppermute | solution.py:21
  42.2 3.8 %collective-permute-done.6 = f32[2,1,3,1152]{3,2,1,0:T(4,128)S(1)} collective-permute-done((f32[2,1,3,1152]{3,2,1,0:T(4,128)S(1)}, f32[2,1,3,1152]{3,2,1,0:T(4,128)S(1)}, u32[]{:S(2)}, u32[]{:S(2)}) %collective-permute-start.6) | collective-permute-done | bytes 27680 | tf_op jit(solution)/shard_map/ppermute | solution.py:24
  48.7 4.3 %collective-permute-start.7 = (f32[2,1,3,1152]{3,2,1,0:T(4,128)S(1)}, f32[2,1,3,1152]{3,2,1,0:T(4,128)S(1)}, u32[]{:S(2)}, u32[]{:S(2)}) collective-permute-start(f32[2,1,3,1152]{3,2,1,0:T(4,128)S(1)} %get-tuple-element.34), channel_id=1, source_target_pairs={{0,4},{4,8},{8,12},{12,16},{16,20},{20,24},{24,28},{1,5},{5,9},{9,... | collective-permute-start | bytes 82952 | tf_op jit(solution)/shard_map/ppermute | solution.py:21
  55.3 4.3 %all-to-all-start.1 = ((f32[4,2,1,48,288]{4,3,1,2,0:T(8,128)}), f32[4,2,1,48,288]{4,3,1,2,0:T(8,128)}, u32[]{:S(2)}, u32[]{:S(2)}) async-start(f32[4,2,1,48,288]{4,3,1,2,0:T(8,128)} %pad_maximum_fusion), calls=%async_computation.1 | async-start | bytes 1179648 | tf_op jit(solution)/shard_map/all_to_all | solution.py:131
  61.6 2.8 %reshape.594 = f32[4,1,27648]{2,1,0:T(1,128)} reshape(f32[1152,1,2,48]{3,2,1,0:T(2,128)S(1)} %bitcast.43) | data formatting | bytes 884736
  64.5 4.5 %all-to-all-done.1 = f32[4,2,1,48,288]{4,3,1,2,0:T(8,128)} async-done(((f32[4,2,1,48,288]{4,3,1,2,0:T(8,128)}), f32[4,2,1,48,288]{4,3,1,2,0:T(8,128)}, u32[]{:S(2)}, u32[]{:S(2)}) %all-to-all-start.1) | async-done | bytes 442400 | tf_op jit(solution)/shard_map/all_to_all | solution.py:131
  69.0 3.5 %all-to-all-start = ((f32[4,1,27648]{2,1,0:T(1,128)}), f32[4,1,27648]{2,1,0:T(1,128)S(1)}, u32[]{:S(2)}, u32[]{:S(2)}) async-start(f32[4,1,27648]{2,1,0:T(1,128)} %reshape.594), calls=%async_computation | async-start | bytes 884736 | tf_op jit(solution)/shard_map/all_to_all | solution.py:129
  72.5 1.6 %reshape.592 = f32[2,4,13824]{2,0,1:T(2,128)S(1)} reshape(f32[2,4,1,48,288]{4,3,0,2,1:T(8,128)} %bitcast.13) | data formatting | bytes 884736 | tf_op jit(solution)/shard_map/reshape;reshape | solution.py:105
  74.1 6.3 %all-to-all-done = f32[4,1,27648]{2,1,0:T(1,128)S(1)} async-done(((f32[4,1,27648]{2,1,0:T(1,128)}), f32[4,1,27648]{2,1,0:T(1,128)S(1)}, u32[]{:S(2)}, u32[]{:S(2)}) %all-to-all-start) | async-done | bytes 442400 | tf_op jit(solution)/shard_map/all_to_all | solution.py:129
  80.9 2.7 %reduce.2 = f32[4,27648]{1,0:T(4,128)} reduce(f32[4,1,27648]{2,1,0:T(1,128)S(1)} %all-to-all-done, f32[]{:T(128)} %broadcast.305), dimensions={1}, to_apply=%all_to_all.27.reduce_sub_computation | reduce | bytes 884740 | tf_op jit(solution)/shard_map/all_to_all | solution.py:129
  83.6 2.9 %reshape.595 = f32[1152,1,2,48]{3,2,1,0:T(2,128)S(1)} reshape(f32[4,27648]{1,0:T(4,128)} %reduce.2) | data formatting | bytes 884736
  87.8 1.5 %reshape.588 = f32[2,4,13824]{2,1,0:T(4,128)S(1)} reshape(f32[2,4,1,48,288]{4,3,1,0,2:T(8,128)} %bitcast.51) | data formatting | bytes 884736 | tf_op jit(solution)/shard_map/reshape | solution.py:105
  93.2 1.3 %add_subtract_fusion = f32[2,4,13824]{2,1,0:T(4,128)} fusion(f32[2,3,13824]{2,1,0:T(4,128)S(1)} %bitcast.55, f32[2,4,13824]{2,1,0:T(4,128)S(1)} %get-tuple-element.7, f32[2,3,13824]{2,1,0:T(4,128)S(1)} %bitcast.50, f32[2,4,13824]{2,0,1:T(2,128)S(1)} %reshape.592), kind=kLoop, calls=%fused_computation.206 | loop fusion | flops 1327104 | bytes 1990656 | tf_op jit(solution)/shard_map/sub | solution.py:96
  94.5 2.3 %reshape.590 = f32[2,4,48,288]{3,2,1,0:T(8,128)} reshape(f32[2,4,13824]{2,1,0:T(4,128)} %add_subtract_fusion) | data formatting | bytes 884736 | tf_op jit(solution)/shard_map/reshape | solution.py:107
  97.9 11.9 %all_to_all.38 = f32[2,4,48,288]{3,2,0,1:T(8,128)S(1)} all-to-all(f32[2,4,48,288]{3,2,0,1:T(8,128)S(1)} %copy.68), channel_id=1, replica_groups=mesh['lat'=8,'lev'=4] {'lev'}, dimensions={1} | all-to-all | bytes 884736 | tf_op jit(solution)/shard_map/all_to_all | solution.py:106
  111.0 1.4 %all_to_all.34 = f32[2,1,48,1152]{3,2,1,0:T(8,128)S(1)} reshape(f32[2,1,48,4,288]{4,3,2,0,1:T(4,128)} %copy.69) | data formatting | bytes 884736 | tf_op jit(solution)/shard_map/all_to_all | solution.py:106
  114.2 4.5 %collective-permute-start.9 = (f32[2,1,3,1152]{3,2,1,0:T(4,128)S(1)}, f32[2,1,3,1152]{3,2,1,0:T(4,128)S(1)}, u32[]{:S(2)}, u32[]{:S(2)}) collective-permute-start(f32[2,1,3,1152]{3,2,1,0:T(4,128)S(1)} %get-tuple-element.30), channel_id=1, source_target_pairs={{0,4},{4,8},{8,12},{12,16},{16,20},{20,24},{24,28},{1,5},{5,9},{9,... | collective-permute-start | bytes 82952 | tf_op jit(solution)/shard_map/ppermute | solution.py:21
  120.1 2.2 %fusion.142 = f32[2,13824]{1,0:T(2,128)S(1)} fusion(f32[2,4,13824]{2,1,0:T(4,128)} %copy-done.4, f32[2,4,13824]{2,1,0:T(4,128)} %copy-done, f32[2,4,13824]{2,1,0:T(4,128)} %copy-done.3, f32[2,4,13824]{2,1,0:T(4,128)S(1)} %get-tuple-element.8, f32[2,4,13824]{2,1,0:T(4,128)} %copy-done.2, f32[2,4,13824]{2,1,0:T(4,128)S(1)} %multiply_multiply_fusion.5), kind=kLoop, calls=%fused_computation.233 | loop fusion | flops 138240 | bytes 774144 | tf_op jit(solution)/shard_map/add | solution.py:97
  123.1 1.5 %collective-permute-done.10 = f32[2,1,3,1152]{3,2,1,0:T(4,128)S(1)} collective-permute-done((f32[2,1,3,1152]{3,2,1,0:T(4,128)S(1)}, f32[2,1,3,1152]{3,2,1,0:T(4,128)S(1)}, u32[]{:S(2)}, u32[]{:S(2)}) %collective-permute-start.10) | collective-permute-done | bytes 27680 | tf_op jit(solution)/shard_map/ppermute | solution.py:24
  (116 shorter events, 37.1 us)
Async XLA Ops:
  0.6 9.1 %copy-start.5 = (f32[1,48,1152]{2,1,0:T(8,128)S(1)}, f32[1,48,1152]{2,1,0:T(8,128)}, u32[]{:S(2)}) copy-start(f32[1,48,1152]{2,1,0:T(8,128)} %param.5) | copy-start | bytes 663556
  0.6 9.0 %copy-start.1 = (f32[2,1,48,1152]{3,2,1,0:T(8,128)S(1)}, f32[2,1,48,1152]{3,2,1,0:T(8,128)}, u32[]{:S(2)}) copy-start(f32[2,1,48,1152]{3,2,1,0:T(8,128)} %param.4) | copy-start | bytes 1327108
  1.8 14.8 %collective-permute-start = (f32[1,1,1152]{2,1,0:T(1,128)S(1)}, f32[1,1,1152]{2,1,0:T(1,128)S(1)}, u32[]{:S(2)}, u32[]{:S(2)}) collective-permute-start(f32[1,1,1152]{2,1,0:T(1,128)S(1)} %slice.702), channel_id=1, source_target_pairs={{0,4},{4,8},{8,12},{12,16},{16,20},{20,24},{24,28},{1,5},{5,9},{9,... | collective-permute-start | bytes 13832 | tf_op jit(solution)/shard_map/ppermute | solution.py:13
  11.5 5.0 %copy-start.6 = (f32[1,48,1152]{2,1,0:T(8,128)S(1)}, f32[1,48,1152]{2,1,0:T(8,128)}, u32[]{:S(2)}) copy-start(f32[1,48,1152]{2,1,0:T(8,128)} %param.6) | copy-start | bytes 663556
  11.7 5.1 %collective-permute-start.1 = (f32[2,1,3,1152]{3,2,1,0:T(4,128)S(1)}, f32[2,1,3,1152]{3,2,1,0:T(4,128)S(1)}, u32[]{:S(2)}, u32[]{:S(2)}) collective-permute-start(f32[2,1,3,1152]{3,2,1,0:T(4,128)S(1)} %get-tuple-element.46), channel_id=1, source_target_pairs={{0,4},{4,8},{8,12},{12,16},{16,20},{20,24},{24,28},{1,5},{5,9},{9,... | collective-permute-start | bytes 82952 | tf_op jit(solution)/shard_map/ppermute | solution.py:21
  15.1 5.9 %collective-permute-start.2 = (f32[2,1,3,1152]{3,2,1,0:T(4,128)S(1)}, f32[2,1,3,1152]{3,2,1,0:T(4,128)S(1)}, u32[]{:S(2)}, u32[]{:S(2)}) collective-permute-start(f32[2,1,3,1152]{3,2,1,0:T(4,128)S(1)} %get-tuple-element.47), channel_id=1, source_target_pairs={{4,0},{8,4},{12,8},{16,12},{20,16},{24,20},{28,24},{5,1},{9,5},{13... | collective-permute-start | bytes 82952 | tf_op jit(solution)/shard_map/ppermute | solution.py:24
  23.5 5.9 %copy-start.7 = (f32[2,1,48,1152]{3,2,1,0:T(8,128)S(1)}, f32[2,1,48,1152]{3,2,1,0:T(8,128)}, u32[]{:S(2)}) copy-start(f32[2,1,48,1152]{3,2,1,0:T(8,128)} %param.7) | copy-start | bytes 1327108
  23.8 6.0 %collective-permute-start.3 = (f32[2,1,3,1152]{3,2,1,0:T(4,128)S(1)}, f32[2,1,3,1152]{3,2,1,0:T(4,128)S(1)}, u32[]{:S(2)}, u32[]{:S(2)}) collective-permute-start(f32[2,1,3,1152]{3,2,1,0:T(4,128)S(1)} %get-tuple-element.42), channel_id=1, source_target_pairs={{0,4},{4,8},{8,12},{12,16},{16,20},{20,24},{24,28},{1,5},{5,9},{9,... | collective-permute-start | bytes 82952 | tf_op jit(solution)/shard_map/ppermute | solution.py:21
  28.1 5.9 %collective-permute-start.4 = (f32[2,1,3,1152]{3,2,1,0:T(4,128)S(1)}, f32[2,1,3,1152]{3,2,1,0:T(4,128)S(1)}, u32[]{:S(2)}, u32[]{:S(2)}) collective-permute-start(f32[2,1,3,1152]{3,2,1,0:T(4,128)S(1)} %get-tuple-element.43), channel_id=1, source_target_pairs={{4,0},{8,4},{12,8},{16,12},{20,16},{24,20},{28,24},{5,1},{9,5},{13... | collective-permute-start | bytes 82952 | tf_op jit(solution)/shard_map/ppermute | solution.py:24
  36.7 5.5 %collective-permute-start.5 = (f32[2,1,3,1152]{3,2,1,0:T(4,128)S(1)}, f32[2,1,3,1152]{3,2,1,0:T(4,128)S(1)}, u32[]{:S(2)}, u32[]{:S(2)}) collective-permute-start(f32[2,1,3,1152]{3,2,1,0:T(4,128)S(1)} %get-tuple-element.38), channel_id=1, source_target_pairs={{0,4},{4,8},{8,12},{12,16},{16,20},{20,24},{24,28},{1,5},{5,9},{9,... | collective-permute-start | bytes 82952 | tf_op jit(solution)/shard_map/ppermute | solution.py:21
  40.1 5.9 %collective-permute-start.6 = (f32[2,1,3,1152]{3,2,1,0:T(4,128)S(1)}, f32[2,1,3,1152]{3,2,1,0:T(4,128)S(1)}, u32[]{:S(2)}, u32[]{:S(2)}) collective-permute-start(f32[2,1,3,1152]{3,2,1,0:T(4,128)S(1)} %get-tuple-element.39), channel_id=1, source_target_pairs={{4,0},{8,4},{12,8},{16,12},{20,16},{24,20},{28,24},{5,1},{9,5},{13... | collective-permute-start | bytes 82952 | tf_op jit(solution)/shard_map/ppermute | solution.py:24
  48.5 5.9 %copy-start.8 = (f32[1,2,1,48,288]{4,3,1,2,0:T(8,128)S(1)}, f32[1,2,1,48,288]{4,3,1,2,0:T(8,128)}, u32[]{:S(2)}) copy-start(f32[1,2,1,48,288]{4,3,1,2,0:T(8,128)} %slice_bitcast_fusion.3) | copy-start | bytes 331780
  48.7 10.9 %collective-permute-start.7 = (f32[2,1,3,1152]{3,2,1,0:T(4,128)S(1)}, f32[2,1,3,1152]{3,2,1,0:T(4,128)S(1)}, u32[]{:S(2)}, u32[]{:S(2)}) collective-permute-start(f32[2,1,3,1152]{3,2,1,0:T(4,128)S(1)} %get-tuple-element.34), channel_id=1, source_target_pairs={{0,4},{4,8},{8,12},{12,16},{16,20},{20,24},{24,28},{1,5},{5,9},{9,... | collective-permute-start | bytes 82952 | tf_op jit(solution)/shard_map/ppermute | solution.py:21
  53.1 6.5 %collective-permute-start.8 = (f32[2,1,3,1152]{3,2,1,0:T(4,128)S(1)}, f32[2,1,3,1152]{3,2,1,0:T(4,128)S(1)}, u32[]{:S(2)}, u32[]{:S(2)}) collective-permute-start(f32[2,1,3,1152]{3,2,1,0:T(4,128)S(1)} %get-tuple-element.35), channel_id=1, source_target_pairs={{4,0},{8,4},{12,8},{16,12},{20,16},{24,20},{28,24},{5,1},{9,5},{13... | collective-permute-start | bytes 82952 | tf_op jit(solution)/shard_map/ppermute | solution.py:24
  55.3 13.7 %all-to-all-start.1 = ((f32[4,2,1,48,288]{4,3,1,2,0:T(8,128)}), f32[4,2,1,48,288]{4,3,1,2,0:T(8,128)}, u32[]{:S(2)}, u32[]{:S(2)}) async-start(f32[4,2,1,48,288]{4,3,1,2,0:T(8,128)} %pad_maximum_fusion), calls=%async_computation.1 | async-start | bytes 1179648 | tf_op jit(solution)/shard_map/all_to_all | solution.py:131
  69.0 11.4 %all-to-all-start = ((f32[4,1,27648]{2,1,0:T(1,128)}), f32[4,1,27648]{2,1,0:T(1,128)S(1)}, u32[]{:S(2)}, u32[]{:S(2)}) async-start(f32[4,1,27648]{2,1,0:T(1,128)} %reshape.594), calls=%async_computation | async-start | bytes 884736 | tf_op jit(solution)/shard_map/all_to_all | solution.py:129
  89.9 0.8 copy-start.2
  91.2 0.8 copy-start.3
  91.9 2.6 %copy-start = (f32[2,4,13824]{2,1,0:T(4,128)}, f32[2,4,13824]{2,1,0:T(4,128)S(1)}, u32[]{:S(2)}) copy-start(f32[2,4,13824]{2,1,0:T(4,128)S(1)} %get-tuple-element.6) | copy-start | bytes 1327108
  92.4 0.8 copy-start.4
  114.2 8.9 %collective-permute-start.9 = (f32[2,1,3,1152]{3,2,1,0:T(4,128)S(1)}, f32[2,1,3,1152]{3,2,1,0:T(4,128)S(1)}, u32[]{:S(2)}, u32[]{:S(2)}) collective-permute-start(f32[2,1,3,1152]{3,2,1,0:T(4,128)S(1)} %get-tuple-element.30), channel_id=1, source_target_pairs={{0,4},{4,8},{8,12},{12,16},{16,20},{20,24},{24,28},{1,5},{5,9},{9,... | collective-permute-start | bytes 82952 | tf_op jit(solution)/shard_map/ppermute | solution.py:21
  118.8 5.9 %collective-permute-start.10 = (f32[2,1,3,1152]{3,2,1,0:T(4,128)S(1)}, f32[2,1,3,1152]{3,2,1,0:T(4,128)S(1)}, u32[]{:S(2)}, u32[]{:S(2)}) collective-permute-start(f32[2,1,3,1152]{3,2,1,0:T(4,128)S(1)} %get-tuple-element.31), channel_id=1, source_target_pairs={{4,0},{8,4},{12,8},{16,12},{20,16},{24,20},{28,24},{5,1},{9,5},{13... | collective-permute-start | bytes 82952 | tf_op jit(solution)/shard_map/ppermute | solution.py:24
